TPU v7x, 512 devices: a whole 4x4x16 slice. The times are simulated.
512 devices in a mesh: ctx: 32 (over x, z_lo), tp: 16 (over y, z_hi, core).
Axes of the slice: x: 4, y: 4, z: 16 (z_hi: 2, z_lo: 8; z = z_hi * 8 + z_lo), core: 2. Of those that a mesh axis runs over, the one named last changes fastest.
Arguments:
- queries: bfloat16 [4096, 4096], P('ctx', 'tp'), may hold values from -5 to 5
- key_states: bfloat16 [4096, 4096], P('ctx', 'tp'), may hold values from -5 to 5
- value_states: bfloat16 [4096, 4096], P('ctx', 'tp'), may hold values from -6 to 6
- attn_output: bfloat16 [4096, 4096], P('ctx', 'tp'), may hold values from -6 to 6
- output_grad: bfloat16 [4096, 4096], P('ctx', 'tp'), may hold values from -6 to 6
- block_map: int32 [32, 32], replicated, may hold values from 0 to 1, as said below
- w_query: bfloat16 [8192, 4096], P('ctx', 'tp'), may hold values from -0.09375 to 0.09375
- w_key: bfloat16 [8192, 4096], P('ctx', 'tp'), may hold values from -0.09375 to 0.09375
- w_value: bfloat16 [8192, 4096], P('ctx', 'tp'), may hold values from -0.09375 to 0.09375
Outputs:
- grad_input: bfloat16 [4096, 8192], P('tp', 'ctx')
Inputs may be any that keep to these rules, and one draw needn't show every extreme that they name: block_map[i, j] is 1 wherever |i - j| <= 1; elsewhere each row is 1 on a share of its entries that differs from row to row.
All inputs are finite; a program needn't handle non-finite values.
Results may differ from a plain program's by a relative error of at most 0.014.
Values may be sent and summed in bfloat16 or wider, within the bound.
No kernel may reach another device: no remote copies, remote signals or barrier semaphores. Data moves between devices by JAX's collectives and lax.ppermute only.
A program may use at most 64 MiB of HBM per device.

v0:
```python
import math
import jax
import jax.numpy as jnp
from jax import lax
from jax.sharding import PartitionSpec as P

HD = 128
BLK = 128
NEG_FILL = -1e30


def block_mask(block_map, row_offset, row_count, col_offset, col_count):
    tiles = lax.dynamic_slice(
        block_map, (row_offset // BLK, col_offset // BLK), (row_count // BLK, col_count // BLK)
    )
    spread = jnp.broadcast_to(
        tiles[:, None, :, None], (row_count // BLK, BLK, col_count // BLK, BLK)
    )
    return spread.reshape(row_count, col_count) > 0


def resolved_rows(values):
    return lax.optimization_barrier(values.astype(jnp.bfloat16)).astype(jnp.float32)


def stat_update(state, query_heads, key_block, allowed, score_scale):
    row_max, row_sum = state
    scores = (
        jnp.einsum("qhd,khd->hqk", query_heads, key_block, preferred_element_type=jnp.float32)
        * score_scale
    )
    masked = jnp.where(allowed[None], scores, NEG_FILL)
    new_max = jnp.maximum(row_max, jnp.max(masked, axis=2))
    kept = jnp.where(allowed[None], jnp.exp(masked - new_max[:, :, None]), 0.0)
    return (new_max, row_sum * jnp.exp(row_max - new_max) + jnp.sum(kept, axis=2))


def gradient_block(
    query_heads, grad_heads, key_block, value_block, log_total, row_delta, allowed, score_scale
):
    scores = (
        jnp.einsum("qhd,khd->hqk", query_heads, key_block, preferred_element_type=jnp.float32)
        * score_scale
    )
    masked = jnp.where(allowed[None], scores, NEG_FILL)
    probs = jnp.where(allowed[None], jnp.exp(masked - log_total[:, :, None]), 0.0)
    probs_low = probs.astype(jnp.bfloat16)
    dprobs = jnp.einsum("qhd,khd->hqk", grad_heads, value_block, preferred_element_type=jnp.float32)
    score_gradient = (probs * (dprobs - row_delta[:, :, None]) * score_scale).astype(jnp.bfloat16)
    return (probs_low, score_gradient)


def per_device(
    queries, key_states, value_states, attn_output, output_grad, block_map, w_query, w_key, w_value
):
    slab_rows, width = queries.shape
    head_count = width // HD
    context_count = lax.axis_size("ctx")
    score_scale = 1.0 / math.sqrt(HD)
    row_offset = lax.axis_index("ctx") * slab_rows
    query_heads = queries.reshape(slab_rows, head_count, HD)
    grad_heads = output_grad.reshape(slab_rows, head_count, HD)
    output_heads = attn_output.reshape(slab_rows, head_count, HD)
    row_delta = jnp.sum(grad_heads.astype(jnp.float32) * output_heads.astype(jnp.float32), axis=2).T
    start_state = (
        jnp.full((head_count, slab_rows), NEG_FILL, jnp.float32),
        jnp.zeros((head_count, slab_rows), jnp.float32),
    )
    key_value = jnp.concatenate([key_states, value_states], axis=1)
    spread = jnp.broadcast_to(key_value[None], (context_count,) + key_value.shape)
    gathered = lax.all_to_all(spread, "ctx", 0, 0, tiled=True).reshape(
        context_count * slab_rows, 2 * width
    )
    full_keys, full_values = (gathered[:, :width], gathered[:, width:])
    group_size = min(context_count, max(1, 512 // slab_rows))
    key_span = slab_rows * group_size
    total_block_count = context_count // group_size
    key_blocks = full_keys.reshape(total_block_count, key_span, head_count, HD)
    value_blocks = full_values.reshape(total_block_count, key_span, head_count, HD)
    block_ids = jnp.arange(total_block_count, dtype=jnp.int32)

    def stat_step(state, inputs):
        key_block, block_index = inputs
        allowed = block_mask(block_map, row_offset, slab_rows, block_index * key_span, key_span)

        def stat_active_step(previous):
            return stat_update(previous, query_heads, key_block, allowed, score_scale)

        return (
            lax.cond(jnp.any(allowed), stat_active_step, lambda previous: previous, state),
            None,
        )

    (row_max, row_sum), _ = lax.scan(stat_step, start_state, (key_blocks, block_ids))
    log_total = row_max + jnp.log(row_sum)

    def back_step(dq_total, inputs):
        key_block, value_block, block_index = inputs
        allowed = block_mask(block_map, row_offset, slab_rows, block_index * key_span, key_span)

        def back_active_step(previous):
            probs_low, score_gradient = gradient_block(
                query_heads,
                grad_heads,
                key_block,
                value_block,
                log_total,
                row_delta,
                allowed,
                score_scale,
            )
            dv_part = jnp.einsum(
                "hqk,qhd->khd", probs_low, grad_heads, preferred_element_type=jnp.float32
            ).astype(jnp.bfloat16)
            dk_part = jnp.einsum(
                "hqk,qhd->khd", score_gradient, query_heads, preferred_element_type=jnp.float32
            ).astype(jnp.bfloat16)
            per_slab = jnp.einsum(
                "hqgk,gkhd->gqhd",
                score_gradient.reshape(head_count, slab_rows, group_size, slab_rows),
                key_block.reshape(group_size, slab_rows, head_count, HD),
                preferred_element_type=jnp.float32,
            )
            joined = jnp.concatenate(
                [dk_part.reshape(key_span, width), dv_part.reshape(key_span, width)], axis=1
            )
            return (previous + jnp.sum(resolved_rows(per_slab), axis=0), joined)

        def empty_step(previous):
            return (previous, jnp.zeros((key_span, 2 * width), jnp.bfloat16))

        return lax.cond(jnp.any(allowed), back_active_step, empty_step, dq_total)

    dq_total, joined_blocks = lax.scan(
        back_step,
        jnp.zeros((slab_rows, head_count, HD), jnp.float32),
        (key_blocks, value_blocks, block_ids),
    )
    local_grads = dq_total.astype(jnp.bfloat16).reshape(slab_rows, width)
    part_grads = joined_blocks.reshape(context_count * slab_rows, 2 * width)
    part_width = part_grads.shape[1]
    arrived = lax.all_to_all(
        part_grads.reshape(context_count, slab_rows, part_width),
        "ctx",
        split_axis=0,
        concat_axis=0,
        tiled=True,
    )
    finished = jnp.sum(arrived.astype(jnp.float32), axis=0).astype(jnp.bfloat16)
    own_grads = jnp.concatenate([local_grads, finished], axis=1)
    gradients = lax.all_gather(own_grads, "ctx", axis=0, tiled=True)
    projections = jnp.concatenate([w_query, w_key, w_value], axis=1)
    return lax.psum_scatter(
        lax.dot_general(
            gradients, projections, (((1,), (1,)), ((), ())), preferred_element_type=jnp.float32
        ).astype(jnp.bfloat16),
        "tp",
        scatter_dimension=0,
        tiled=True,
    )


def solution(mesh):
    return jax.shard_map(
        per_device,
        mesh=mesh,
        in_specs=(
            P("ctx", "tp"),
            P("ctx", "tp"),
            P("ctx", "tp"),
            P("ctx", "tp"),
            P("ctx", "tp"),
            P(),
            P("ctx", "tp"),
            P("ctx", "tp"),
            P("ctx", "tp"),
        ),
        out_specs=P("tp", "ctx"),
        check_vma=False,
    )
```

profile of v0, /device:TPU:2, one launch (start us, length us, event | category | flops | bytes accessed | tf_op | source)
XLA Modules:
  0.0 892.0 jit_solution(6560580829469173553)
XLA Ops:
  7.5 2.9 broadcast_in_dim.103
  10.4 15.9 %all-to-all-start = ((bf16[32,128,512]{1,2,0:T(8,128)(2,1)}), bf16[32,128,512]{1,2,0:T(8,128)(2,1)}, u32[]{:S(2)}, u32[]{:S(2)}) async-start(bf16[32,128,512]{1,2,0:T(8,128)(2,1)} %broadcast_in_dim.103), calls=%async_computation | async-start | bytes 8388608 | tf_op jit(solution)/shard_map/all_to_all | solution.py:71
  26.9 174.6 %all-to-all-done = bf16[32,128,512]{1,2,0:T(8,128)(2,1)} async-done(((bf16[32,128,512]{1,2,0:T(8,128)(2,1)}), bf16[32,128,512]{1,2,0:T(8,128)(2,1)}, u32[]{:S(2)}, u32[]{:S(2)}) %all-to-all-start) | async-done | bytes 4194336 | tf_op jit(solution)/shard_map/all_to_all | solution.py:71
  201.5 6.5 copy.66
  208.0 3.8 fusion.27
  211.8 2.1 reshape.89
  215.9 30.8 %while.33 = (s32[]{:T(128)}, f32[2,128]{1,0:T(2,128)S(1)}, f32[2,128]{1,0:T(2,128)S(1)}, s32[8]{0:T(128)S(1)}, s32[32,32]{1,0:T(8,128)}, /*index=5*/s32[]{:T(128...) while((s32[]{:T(128)}, f32[2,128]{1,0:T(2,128)S(1)}, ...), condition=%wide.region_6.7_spmd, body=%wide.region_0.6_spmd.sunk | while | flops 34406940 | bytes 1391623 | solution.py:94
  246.7 4.0 reshape.90
  250.7 3.3 copy.75
  254.1 54.5 %while.34 = (s32[]{:T(128)}, f32[128,2,128]{2,0,1:T(8,128)S(1)}, bf16[8,512,512]{2,1,0:T(8,128)(2,1)}, s32[8]{0:T(128)S(1)}, s32[32,32]{1,0:T(8,128)}, /*index=5...) while((s32[]{:T(128)}, f32[128,2,128]{2,0,1:T(8,128)S(1)}, ...), condition=%wide.region_13.14_spmd, body=%wide.region_8.13_spmd.sunk | while | flops 170721312 | bytes 8655399 | solution.py:134
  257.4 2.5 conditional.5
  264.2 2.5 conditional.5
  271.0 2.5 conditional.5
  277.8 2.5 conditional.5
  284.6 2.5 conditional.5
  291.4 2.5 conditional.5
  298.2 2.5 conditional.5
  305.0 2.5 conditional.5
  308.5 18.0 %all-to-all-start.1 = ((bf16[32,128,512]{2,1,0:T(8,128)(2,1)}), bf16[32,128,512]{2,1,0:T(8,128)(2,1)}, u32[]{:S(2)}, u32[]{:S(2)}) async-start(bf16[32,128,512]{2,1,0:T(8,128)(2,1)} %bitcast.65), calls=%async_computation.1 | async-start | bytes 8388608 | tf_op jit(solution)/shard_map/all_to_all | solution.py:142
  326.8 175.0 %all-to-all-done.1 = bf16[32,128,512]{2,1,0:T(8,128)(2,1)} async-done(((bf16[32,128,512]{2,1,0:T(8,128)(2,1)}), bf16[32,128,512]{2,1,0:T(8,128)(2,1)}, u32[]{:S(2)}, u32[]{:S(2)}) %all-to-all-start.1) | async-done | bytes 4194336 | tf_op jit(solution)/shard_map/all_to_all | solution.py:142
  501.9 2.8 reduce_sum.43
  505.4 236.3 %all-gather.2.cloned.1.call-done = bf16[4096,768]{1,0:T(8,128)(2,1)} async-done(((bf16[128,768]{1,0:T(8,128)(2,1)}), bf16[4096,768]{1,0:T(8,128)(2,1)}) %all-gather.2.cloned.1.call-update) | async-done | bytes 6291472 | tf_op jit(solution)/shard_map/all_gather | solution.py:151
  741.7 6.0 convolution_convert_fusion.3
  747.7 137.5 %reduce-scatter.2.cloned.1.call-done = bf16[256,256]{1,0:T(8,128)(2,1)} async-done(((bf16[4096,256]{1,0:T(8,128)(2,1)}), bf16[256,256]{1,0:T(8,128)(2,1)}) %reduce-scatter.2.cloned.1.call-update) | async-done | bytes 131088 | tf_op jit(solution)/shard_map/reduce_scatter | solution.py:153
  (250 shorter events, 74.1 us)
Async XLA Ops:
  10.4 15.9 %copy-start.1 = (bf16[128,256]{1,0:T(8,128)(2,1)S(1)}, bf16[128,256]{1,0:T(8,128)(2,1)}, u32[]{:S(2)}) copy-start(bf16[128,256]{1,0:T(8,128)(2,1)} %param.17) | copy-start | bytes 196612
  10.4 16.2 %copy-start.2 = (bf16[128,256]{1,0:T(8,128)(2,1)S(1)}, bf16[128,256]{1,0:T(8,128)(2,1)}, u32[]{:S(2)}) copy-start(bf16[128,256]{1,0:T(8,128)(2,1)} %param.21) | copy-start | bytes 196612
  10.4 16.3 %copy-start = (bf16[128,256]{1,0:T(8,128)(2,1)S(1)}, bf16[128,256]{1,0:T(8,128)(2,1)}, u32[]{:S(2)}) copy-start(bf16[128,256]{1,0:T(8,128)(2,1)} %param.20) | copy-start | bytes 196612
  10.4 191.0 %all-to-all-start = ((bf16[32,128,512]{1,2,0:T(8,128)(2,1)}), bf16[32,128,512]{1,2,0:T(8,128)(2,1)}, u32[]{:S(2)}, u32[]{:S(2)}) async-start(bf16[32,128,512]{1,2,0:T(8,128)(2,1)} %broadcast_in_dim.103), calls=%async_computation | async-start | bytes 8388608 | tf_op jit(solution)/shard_map/all_to_all | solution.py:71
  308.5 193.3 %all-to-all-start.1 = ((bf16[32,128,512]{2,1,0:T(8,128)(2,1)}), bf16[32,128,512]{2,1,0:T(8,128)(2,1)}, u32[]{:S(2)}, u32[]{:S(2)}) async-start(bf16[32,128,512]{2,1,0:T(8,128)(2,1)} %bitcast.65), calls=%async_computation.1 | async-start | bytes 8388608 | tf_op jit(solution)/shard_map/all_to_all | solution.py:142
  326.5 415.2 %copy-start.3 = (bf16[256,256]{1,0:T(8,128)(2,1)S(1)}, bf16[256,256]{1,0:T(8,128)(2,1)}, u32[]{:S(2)}) copy-start(bf16[256,256]{1,0:T(8,128)(2,1)} %param.25) | copy-start | bytes 393220
  326.5 415.2 %copy-start.4 = (bf16[256,256]{1,0:T(8,128)(2,1)S(1)}, bf16[256,256]{1,0:T(8,128)(2,1)}, u32[]{:S(2)}) copy-start(bf16[256,256]{1,0:T(8,128)(2,1)} %param.24) | copy-start | bytes 393220
  326.5 415.2 %copy-start.5 = (bf16[256,256]{1,0:T(8,128)(2,1)S(1)}, bf16[256,256]{1,0:T(8,128)(2,1)}, u32[]{:S(2)}) copy-start(bf16[256,256]{1,0:T(8,128)(2,1)} %param.23) | copy-start | bytes 393220
  326.5 415.2 %all-gather.2.cloned.1.call-start = ((), (), s32[]{:S(2)}) async-start(), calls=%async_computation.3 | async-start | bytes 6488064 | tf_op jit(solution)/shard_map/all_gather | solution.py:151
  505.4 379.8 %reduce-scatter.2.cloned.1.call-start = ((), (), s32[]{:S(2)}) async-start(), calls=%async_computation.4 | async-start | bytes 2228224 | tf_op jit(solution)/shard_map/reduce_scatter | solution.py:153
Sparse Core Ops, SparseCore 0:
  505.5 236.1 all-gather.1
  747.8 137.2 reduce-scatter.1
where the time goes:
time: 894 us; the launch traced here: 892 us
  waiting for transfers between devices  723 us (81%)
  local copies, waits for them, and re-layouts  44.4 us (5%)
  starting transfers between devices  33.9 us (4%)
  other arithmetic  31.2 us (3%)
  matrix products  25.4 us (3%)
  loops' own time  20.1 us (2%)
  between operations  13.6 us (2%)
    all_gather x1, waiting for transfers between devices, per_device(): gradients = lax.all_gather(own_grads, 'ctx', axis=0, tiled=True)  236 us
    all_to_all x1, waiting for transfers between devices, per_device(): lax.all_to_all(part_grads.reshape(context_count, slab_rows, part_width),...  175 us
    all_to_all x1, waiting for transfers between devices, per_device(): lax.all_to_all(spread, 'ctx', 0, 0, tiled=True)  175 us
    reduce_scatter x1, waiting for transfers between devices, per_device(): lax.psum_scatter(lax.dot_general(gradients, projections, (((1,), (1,)), (...  137 us
    all_to_all x1, starting transfers between devices, per_device(): lax.all_to_all(part_grads.reshape(context_count, slab_rows, part_width),...  18 us
  transfers between devices with their start and end apart: 4, of which 4 were waited for; matrix products, arithmetic and copies ran while one was open for 0% of the time, Pallas kernels for 0%

commit v1 on v0

--- a/solution.py
+++ b/solution.py
@@ -148,7 +148,10 @@
     )
     finished = jnp.sum(arrived.astype(jnp.float32), axis=0).astype(jnp.bfloat16)
     own_grads = jnp.concatenate([local_grads, finished], axis=1)
-    gradients = lax.all_gather(own_grads, "ctx", axis=0, tiled=True)
+    n_dev = lax.axis_size("ctx")
+    parts = jnp.stack([own_grads for _ in range(n_dev)])
+    parts = lax.all_to_all(parts, "ctx", split_axis=0, concat_axis=0)
+    gradients = jnp.concatenate(parts, axis=0)
     projections = jnp.concatenate([w_query, w_key, w_value], axis=1)
     return lax.psum_scatter(
         lax.dot_general(

time: 894 us -> 933 us (1.044)
  blocking collectives: 0 us -> 291 us
  waiting for transfers between devices: 723 us -> 471 us
    all_to_all x0 -> x1, blocking collectives: none -> 291 us  [per_device(): parts = lax.all_to_all(parts, 'ctx', split_axis=0, concat_axis=0)]
    all_gather x1 -> x0, waiting for transfers between devices: 236 us -> none  [per_device(): gradients = lax.all_gather(own_grads, 'ctx', axis=0, tiled=True)]
    reduce_scatter x1, waiting for transfers between devices: 137 us -> 122 us  [per_device(): lax.psum_scatter(lax.dot_general(gradients, projections, (((1,), (1,)), (...]
  transfers between devices with their start and end apart: 4 -> 3, of which waited for: 4 -> 3; matrix products, arithmetic and copies ran while one was open for 0% -> 0% of each run, Pallas kernels for 0% -> 0%
where the time goes in v1:
time: 933 us; the launch traced here: 931 us
  waiting for transfers between devices  471 us (50%)
  blocking collectives  291 us (31%)
  local copies, waits for them, and re-layouts  45.8 us (5%)
  starting transfers between devices  33.9 us (4%)
  other arithmetic  31.1 us (3%)
  matrix products  22.6 us (2%)
  loops' own time  22.3 us (2%)
  between operations  13.6 us (1%)
    all_to_all x1, blocking collectives, per_device(): parts = lax.all_to_all(parts, 'ctx', split_axis=0, concat_axis=0)  291 us
    all_to_all x1, waiting for transfers between devices, per_device(): lax.all_to_all(part_grads.reshape(context_count, slab_rows, part_width),...  175 us
    all_to_all x1, waiting for transfers between devices, per_device(): lax.all_to_all(spread, 'ctx', 0, 0, tiled=True)  175 us
    reduce_scatter x1, waiting for transfers between devices, per_device(): lax.psum_scatter(lax.dot_general(gradients, projections, (((1,), (1,)), (...  122 us
  transfers between devices with their start and end apart: 3, of which 3 were waited for; matrix products, arithmetic and copies ran while one was open for 0% of the time, Pallas kernels for 0%

profile of v1, /device:TPU:2, one launch (start us, length us, event | category | flops | bytes accessed | tf_op | source)
XLA Modules:
  0.0 931.2 jit_solution(1967418325772480129)
XLA Ops:
  7.5 2.9 broadcast_in_dim.103
  10.5 15.9 %all-to-all-start = ((bf16[32,128,512]{1,2,0:T(8,128)(2,1)}), bf16[32,128,512]{1,2,0:T(8,128)(2,1)}, u32[]{:S(2)}, u32[]{:S(2)}) async-start(bf16[32,128,512]{1,2,0:T(8,128)(2,1)} %broadcast_in_dim.103), calls=%async_computation | async-start | bytes 8388608 | tf_op jit(solution)/shard_map/all_to_all | solution.py:71
  26.9 174.6 %all-to-all-done = bf16[32,128,512]{1,2,0:T(8,128)(2,1)} async-done(((bf16[32,128,512]{1,2,0:T(8,128)(2,1)}), bf16[32,128,512]{1,2,0:T(8,128)(2,1)}, u32[]{:S(2)}, u32[]{:S(2)}) %all-to-all-start) | async-done | bytes 4194336 | tf_op jit(solution)/shard_map/all_to_all | solution.py:71
  201.5 6.5 copy.66
  208.0 3.8 fusion.27
  211.9 2.1 reshape.95
  216.0 32.5 %while.33 = (s32[]{:T(128)}, f32[2,128]{1,0:T(2,128)S(1)}, f32[2,128]{1,0:T(2,128)S(1)}, s32[8]{0:T(128)S(1)}, s32[32,32]{1,0:T(8,128)}, /*index=5*/s32[]{:T(128...) while((s32[]{:T(128)}, f32[2,128]{1,0:T(2,128)S(1)}, ...), condition=%wide.region_6.7_spmd, body=%wide.region_0.6_spmd.sunk | while | flops 34406940 | bytes 1391623 | solution.py:94
  248.5 4.0 reshape.96
  252.4 3.3 copy.75
  255.8 56.2 %while.34 = (s32[]{:T(128)}, f32[128,2,128]{2,0,1:T(8,128)S(1)}, bf16[8,512,512]{2,1,0:T(8,128)(2,1)}, s32[8]{0:T(128)S(1)}, s32[32,32]{1,0:T(8,128)}, /*index=5...) while((s32[]{:T(128)}, f32[128,2,128]{2,0,1:T(8,128)S(1)}, ...), condition=%wide.region_13.14_spmd, body=%wide.region_8.13_spmd.sunk | while | flops 170721312 | bytes 8655399 | solution.py:134
  259.3 2.5 conditional.5
  266.3 2.5 conditional.5
  273.3 2.5 conditional.5
  280.4 2.5 conditional.5
  287.4 2.5 conditional.5
  294.4 2.5 conditional.5
  301.5 2.5 conditional.5
  308.5 2.5 conditional.5
  312.0 18.0 %all-to-all-start.1 = ((bf16[32,128,512]{2,1,0:T(8,128)(2,1)}), bf16[32,128,512]{2,1,0:T(8,128)(2,1)}, u32[]{:S(2)}, u32[]{:S(2)}) async-start(bf16[32,128,512]{2,1,0:T(8,128)(2,1)} %bitcast.67), calls=%async_computation.1 | async-start | bytes 8388608 | tf_op jit(solution)/shard_map/all_to_all | solution.py:142
  330.3 175.1 %all-to-all-done.1 = bf16[32,128,512]{2,1,0:T(8,128)(2,1)} async-done(((bf16[32,128,512]{2,1,0:T(8,128)(2,1)}), bf16[32,128,512]{2,1,0:T(8,128)(2,1)}, u32[]{:S(2)}, u32[]{:S(2)}) %all-to-all-start.1) | async-done | bytes 4194336 | tf_op jit(solution)/shard_map/all_to_all | solution.py:142
  505.3 2.8 reduce_sum.43
  508.9 290.7 %all_to_all.15 = bf16[32,128,768]{2,1,0:T(8,128)(2,1)S(1)} all-to-all(bf16[32,128,768]{2,1,0:T(8,128)(2,1)S(1)} %stack.2), channel_id=1, replica_groups=mesh['ctx'=32,'tp'=16] {'ctx'}, dimensions={0} | all-to-all | bytes 12582912 | tf_op jit(solution)/shard_map/all_to_all | solution.py:153
  799.6 3.2 convolution_convert_fusion.3
  802.8 121.6 %reduce-scatter.2.cloned.1.call-done = bf16[256,256]{1,0:T(8,128)(2,1)} async-done(((bf16[4096,256]{1,0:T(8,128)(2,1)}), bf16[256,256]{1,0:T(8,128)(2,1)}) %reduce-scatter.2.cloned.1.call-update) | async-done | bytes 131088 | tf_op jit(solution)/shard_map/reduce_scatter | solution.py:156
  (249 shorter events, 75.3 us)
Async XLA Ops:
  10.5 15.9 %copy-start.1 = (bf16[128,256]{1,0:T(8,128)(2,1)S(1)}, bf16[128,256]{1,0:T(8,128)(2,1)}, u32[]{:S(2)}) copy-start(bf16[128,256]{1,0:T(8,128)(2,1)} %param.17) | copy-start | bytes 196612
  10.5 16.2 %copy-start.2 = (bf16[128,256]{1,0:T(8,128)(2,1)S(1)}, bf16[128,256]{1,0:T(8,128)(2,1)}, u32[]{:S(2)}) copy-start(bf16[128,256]{1,0:T(8,128)(2,1)} %param.21) | copy-start | bytes 196612
  10.5 16.3 %copy-start = (bf16[128,256]{1,0:T(8,128)(2,1)S(1)}, bf16[128,256]{1,0:T(8,128)(2,1)}, u32[]{:S(2)}) copy-start(bf16[128,256]{1,0:T(8,128)(2,1)} %param.20) | copy-start | bytes 196612
  10.5 191.0 %all-to-all-start = ((bf16[32,128,512]{1,2,0:T(8,128)(2,1)}), bf16[32,128,512]{1,2,0:T(8,128)(2,1)}, u32[]{:S(2)}, u32[]{:S(2)}) async-start(bf16[32,128,512]{1,2,0:T(8,128)(2,1)} %broadcast_in_dim.103), calls=%async_computation | async-start | bytes 8388608 | tf_op jit(solution)/shard_map/all_to_all | solution.py:71
  312.0 193.3 %all-to-all-start.1 = ((bf16[32,128,512]{2,1,0:T(8,128)(2,1)}), bf16[32,128,512]{2,1,0:T(8,128)(2,1)}, u32[]{:S(2)}, u32[]{:S(2)}) async-start(bf16[32,128,512]{2,1,0:T(8,128)(2,1)} %bitcast.67), calls=%async_computation.1 | async-start | bytes 8388608 | tf_op jit(solution)/shard_map/all_to_all | solution.py:142
  330.0 594.4 %reduce-scatter.2.cloned.1.call-start = ((), (), s32[]{:S(2)}) async-start(), calls=%async_computation.4 | async-start | bytes 2228224 | tf_op jit(solution)/shard_map/reduce_scatter | solution.py:156
  508.9 290.7 %copy-start.3 = (bf16[256,256]{1,0:T(8,128)(2,1)S(1)}, bf16[256,256]{1,0:T(8,128)(2,1)}, u32[]{:S(2)}) copy-start(bf16[256,256]{1,0:T(8,128)(2,1)} %param.25) | copy-start | bytes 393220
  508.9 290.7 %copy-start.4 = (bf16[256,256]{1,0:T(8,128)(2,1)S(1)}, bf16[256,256]{1,0:T(8,128)(2,1)}, u32[]{:S(2)}) copy-start(bf16[256,256]{1,0:T(8,128)(2,1)} %param.24) | copy-start | bytes 393220
  508.9 290.7 %copy-start.5 = (bf16[256,256]{1,0:T(8,128)(2,1)S(1)}, bf16[256,256]{1,0:T(8,128)(2,1)}, u32[]{:S(2)}) copy-start(bf16[256,256]{1,0:T(8,128)(2,1)} %param.23) | copy-start | bytes 393220
Sparse Core Ops, SparseCore 0:
  802.9 121.4 reduce-scatter.1
